TPU v7x, 32 devices: a whole 2x2x4 slice. The times are simulated.
32 devices in a mesh: fsdp: 4 (over z), lat: 8 (over y, x, core).
Axes of the slice: x: 2, y: 2, z: 4, core: 2. Of those that a mesh axis runs over, the one named last changes fastest.
Arguments:
- fields: bfloat16 [4, 128, 360, 192], P('fsdp', 'lat'), may hold values from -6 to 6
- cotangent: bfloat16 [4, 128, 360, 192], P('fsdp', 'lat'), may hold values from -6 to 6
- kernel_one: bfloat16 [3, 3, 192, 192], P(None, None, None, 'fsdp'), may hold values from -0.15625 to 0.15625
- kernel_two: bfloat16 [3, 3, 192, 192], P(None, None, None, 'fsdp'), may hold values from -0.15625 to 0.15625
Outputs:
- block_out: bfloat16 [4, 128, 360, 192], P('fsdp', 'lat')
- field_grad: bfloat16 [4, 128, 360, 192], P('fsdp', 'lat')
- grad_one: float32 [3, 3, 192, 192], P(None, None, None, 'fsdp')
- grad_two: float32 [3, 3, 192, 192], P(None, None, None, 'fsdp')
All inputs are finite; a program needn't handle non-finite values.
Results may differ from a plain program's by a relative error of at most 0.0033.
Values may be sent and summed in bfloat16 or wider, within the bound.
No kernel may reach another device: no remote copies, remote signals or barrier semaphores. Data moves between devices by JAX's collectives and lax.ppermute only.
A program may use at most 128 MiB of HBM per device.

v0:
```python
import jax
import jax.numpy as jnp
from jax import lax
from jax.sharding import PartitionSpec as P


def extended(cells, sides, width):
    for axis, dim in sides:
        count = lax.axis_size(axis)
        ends = count - 1
        head = lax.slice_in_dim(cells, 0, width, axis=dim)
        tail = lax.slice_in_dim(cells, cells.shape[dim] - width, cells.shape[dim], axis=dim)
        cells = jnp.concatenate(
            [
                lax.ppermute(tail, axis, [(i, (i + 1) % count) for i in range(ends)]),
                cells,
                lax.ppermute(head, axis, [((i + 1) % count, i) for i in range(ends)]),
            ],
            axis=dim,
        )
    return cells


def wrap_longitude(values):
    return jnp.concatenate([values[:, :, -2:], values, values[:, :, :2]], axis=2)


def padded_rows(values):
    return wrap_longitude(extended(values, (("lat", 1),), 2))


def correlate(padded, kernel):
    return lax.conv_general_dilated(
        padded,
        kernel,
        (1, 1),
        "VALID",
        rhs_dilation=(2, 2),
        dimension_numbers=("NHWC", "HWIO", "NHWC"),
        preferred_element_type=jnp.float32,
    )


def adjoint_kernel(kernel):
    return jnp.transpose(kernel[::-1, ::-1], (0, 1, 3, 2))


def normal_cdf(values):
    return 0.5 * (1.0 + jax.scipy.special.erf(values * 0.7071067811865476))


def kernel_terms(padded, grad_field, height, width_cells):
    return jnp.stack(
        [
            jnp.stack(
                [
                    jnp.einsum(
                        "nhwc,nhwd->cd",
                        padded[:, 2 * a : 2 * a + height, 2 * b : 2 * b + width_cells],
                        grad_field,
                        preferred_element_type=jnp.float32,
                    )
                    for b in range(3)
                ]
            )
            for a in range(3)
        ]
    )


def per_device(fields, cotangent, kernel_one, kernel_two):
    height = fields.shape[1]
    width_cells = fields.shape[2]
    cell_count = (
        lax.axis_size("fsdp") * fields.shape[0] * lax.axis_size("lat") * height * width_cells
    )
    factor = 1.0 / jnp.sqrt(jnp.float32(cell_count))
    full_one, full_two = (
        lax.all_gather(kernel_one, "fsdp", axis=3, tiled=True),
        lax.all_gather(kernel_two, "fsdp", axis=3, tiled=True),
    )
    source_pad = padded_rows(fields)
    preact = correlate(source_pad, full_one)
    hidden = (preact * normal_cdf(preact)).astype(jnp.bfloat16)
    hidden_pad = padded_rows(hidden)
    block_out = (fields.astype(jnp.float32) + correlate(hidden_pad, full_two)).astype(jnp.bfloat16)
    back = correlate(padded_rows(cotangent), adjoint_kernel(full_two))
    slope = normal_cdf(preact) + preact * jnp.exp(-0.5 * preact * preact) * 0.3989422804014327
    inner_grad = (back * slope).astype(jnp.bfloat16)
    field_grad = (
        cotangent.astype(jnp.float32) + correlate(padded_rows(inner_grad), adjoint_kernel(full_one))
    ).astype(jnp.bfloat16)
    terms_two = kernel_terms(hidden_pad, cotangent, height, width_cells) * factor
    terms_one = kernel_terms(source_pad, inner_grad, height, width_cells) * factor
    share_one, share_two = (
        lax.psum_scatter(terms_one, "fsdp", scatter_dimension=3, tiled=True),
        lax.psum_scatter(terms_two, "fsdp", scatter_dimension=3, tiled=True),
    )
    grad_one, grad_two = lax.psum((share_one, share_two), "lat")
    return (block_out, field_grad, grad_one, grad_two)


def solution(mesh):
    placed = (
        P("fsdp", "lat", None, None),
        P("fsdp", "lat", None, None),
        P(None, None, None, "fsdp"),
        P(None, None, None, "fsdp"),
    )
    return jax.shard_map(
        per_device,
        mesh=mesh,
        in_specs=placed,
        out_specs=(
            P("fsdp", "lat", None, None),
            P("fsdp", "lat", None, None),
            P(None, None, None, "fsdp"),
            P(None, None, None, "fsdp"),
        ),
        check_vma=False,
    )
```

profile of v0, /device:TPU:0, one launch (start us, length us, event | category | flops | bytes accessed | tf_op | source)
XLA Modules:
  0.0 521.3 jit_solution(12465785678488781029)
XLA Ops:
  16.7 5.2 %collective-permute-start.4 = (bf16[1,2,360,192]{2,3,1,0:T(8,128)(2,1)}, bf16[1,2,360,192]{2,3,1,0:T(8,128)(2,1)S(1)}, u32[]{:S(2)}, u32[]{:S(2)}) collective-permute-start(bf16[1,2,360,192]{2,3,1,0:T(8,128)(2,1)} %get-tuple-element.33), channel_id=1, source_target_pairs={{0,1},{1,2},{2,3},{3,4},{4,5},{5,6},{6,7},{8,9},{9,10},{10,11},{11... | collective-permute-start | bytes 829448 | tf_op jit(solution)/shard_map/ppermute | solution.py:15
  21.9 21.1 %all_gather.6 = bf16[3,3,192,192]{2,3,1,0:T(8,128)(2,1)} all-gather(bf16[3,3,192,48]{2,3,1,0:T(8,128)(2,1)} %param.6), channel_id=1, replica_groups=mesh['fsdp'=4,'lat'=8] {'fsdp'}, dimensions={3}, use_global_device_ids=true | all-gather | bytes 829440 | tf_op jit(solution)/shard_map/all_gather | solution.py:79
  43.0 4.9 copy.44
  52.7 20.2 %all_gather.7 = bf16[3,3,192,192]{2,3,1,0:T(8,128)(2,1)} all-gather(bf16[3,3,192,48]{2,3,1,0:T(8,128)(2,1)} %param.7), channel_id=1, replica_groups=mesh['fsdp'=4,'lat'=8] {'fsdp'}, dimensions={3}, use_global_device_ids=true | all-gather | bytes 829440 | tf_op jit(solution)/shard_map/all_gather | solution.py:80
  83.0 11.5 %reshape.194 = bf16[20,1,8,46,192]{3,2,4,0,1:T(8,128)(2,1)} reshape(bf16[20,1,368,192]{2,3,0,1:T(8,128)(2,1)} %pad) | data formatting | bytes 5652480 | tf_op jit(solution)/shard_map/conv_general_dilated | solution.py:33
  94.6 11.8 %copy.47 = bf16[20,1,8,46,192]{4,2,3,0,1:T(8,128)(2,1)} copy(bf16[20,1,8,46,192]{3,2,4,0,1:T(8,128)(2,1)} %reshape.194) | data formatting | bytes 5652480 | tf_op jit(solution)/shard_map/conv_general_dilated | solution.py:33
  107.4 8.6 %reshape.196 = bf16[20,1,8,46,192]{3,2,4,0,1:T(8,128)(2,1)} reshape(bf16[20,1,368,192]{2,3,0,1:T(8,128)(2,1)S(1)} %pad.4) | data formatting | bytes 5652480 | tf_op jit(solution)/shard_map/conv_general_dilated | solution.py:33
  116.0 11.8 %copy.61 = bf16[20,1,8,46,192]{4,2,3,0,1:T(8,128)(2,1)} copy(bf16[20,1,8,46,192]{3,2,4,0,1:T(8,128)(2,1)} %reshape.196) | data formatting | bytes 5652480 | tf_op jit(solution)/shard_map/conv_general_dilated | solution.py:33
  128.9 12.3 %multiply_convert_fusion = (bf16[16,8,46,192]{3,1,2,0:T(8,128)(2,1)}, f32[16,8,46,192]{3,1,2,0:T(8,128)S(1)}) fusion(pred[8,46]{0,1:T(8,128)(4,1)S(1)} %copy-done.35, bf16[3,3,192,192]{2,3,1,0:T(8,128)(2,1)S(1)} %copy-done.20, bf16[20,1,7,4,192]{4,2,3,0,1:T(8,128)(2,1)S(1)} %slice.162, bf16[20,1,8,46,192]{4,2,3,0,1:T(8,128)(2,1)} %copy.47), kind=kOutput, calls=%fused_computation.12 | convolution fusion | flops 3922993152 | bytes 10488176 | tf_op jit(solution)/shard_map/conv_general_dilated | solution.py:33
  141.2 10.5 %fusion.9 = bf16[16,8,46,192]{3,1,2,0:T(8,128)(2,1)S(1)} fusion(f32[16,8,46,192]{3,1,2,0:T(8,128)S(1)} %get-tuple-element.37, pred[8,46]{0,1:T(8,128)(4,1)S(1)} %copy-done.35, bf16[3,3,192,192]{2,3,1,0:T(8,128)(2,1)S(1)} %copy-done.22, bf16[20,1,7,4,192]{4,2,3,0,1:T(8,128)(2,1)S(1)} %slice.172, bf16[20,1,8,46,192]{4,2,3,0,1:T(8,128)(2,1)S(1)} %copy-done.15), kind=kOutput, calls=%fused_computation.11 | convolution fusion | flops 3929776128 | bytes 10488176 | tf_op jit(solution)/shard_map/conv_general_dilated | solution.py:33
  221.9 4.7 maximum_maximum_fusion
  232.9 5.0 fusion.43
  254.0 8.6 %reshape.195 = bf16[20,1,8,46,192]{3,2,4,0,1:T(8,128)(2,1)} reshape(bf16[20,1,368,192]{2,3,0,1:T(8,128)(2,1)S(1)} %copy-done.11) | data formatting | bytes 5652480 | tf_op jit(solution)/shard_map/conv_general_dilated | solution.py:33
  262.6 11.8 %copy.56 = bf16[20,1,8,46,192]{4,2,3,0,1:T(8,128)(2,1)} copy(bf16[20,1,8,46,192]{3,2,4,0,1:T(8,128)(2,1)} %reshape.195) | data formatting | bytes 5652480 | tf_op jit(solution)/shard_map/conv_general_dilated | solution.py:33
  275.7 9.7 %broadcast_select_fusion.1 = f32[16,8,46,192]{3,1,2,0:T(8,128)S(1)} fusion(pred[8,46]{0,1:T(8,128)(4,1)S(1)} %copy-done.35, bf16[3,3,192,192]{2,3,1,0:T(8,128)(2,1)S(1)} %copy-done.23, bf16[20,1,7,4,192]{4,2,3,0,1:T(8,128)(2,1)S(1)} %slice.168, bf16[20,1,8,46,192]{4,2,3,0,1:T(8,128)(2,1)} %copy.56), kind=kOutput, calls=%fused_computation.49 | convolution fusion | flops 3917340672 | bytes 8227184 | tf_op jit(solution)/shard_map/conv_general_dilated | solution.py:33
  291.6 4.9 copy.75
  296.5 8.6 %reshape.197 = bf16[20,1,8,46,192]{3,2,4,0,1:T(8,128)(2,1)} reshape(bf16[20,1,368,192]{2,3,0,1:T(8,128)(2,1)S(1)} %copy-done.10) | data formatting | bytes 5652480 | tf_op jit(solution)/shard_map/conv_general_dilated | solution.py:33
  305.0 12.0 %copy.70 = bf16[20,1,8,46,192]{4,2,3,0,1:T(8,128)(2,1)} copy(bf16[20,1,8,46,192]{3,2,4,0,1:T(8,128)(2,1)} %reshape.197) | data formatting | bytes 5652480 | tf_op jit(solution)/shard_map/conv_general_dilated | solution.py:33
  318.2 9.1 %broadcast_select_fusion = f32[16,8,46,192]{3,1,2,0:T(8,128)S(1)} fusion(pred[8,46]{0,1:T(8,128)(4,1)S(1)} %copy-done.35, bf16[3,3,192,192]{2,3,1,0:T(8,128)(2,1)S(1)} %copy-done.21, bf16[20,1,7,4,192]{4,2,3,0,1:T(8,128)(2,1)S(1)} %slice.178, bf16[20,1,8,46,192]{4,2,3,0,1:T(8,128)(2,1)} %copy.70), kind=kOutput, calls=%fused_computation.48 | convolution fusion | flops 3917340672 | bytes 8227184 | tf_op jit(solution)/shard_map/conv_general_dilated | solution.py:33
  327.2 6.1 %copy.71 = f32[16,8,46,192]{3,0,2,1:T(8,128)} copy(f32[16,8,46,192]{3,1,2,0:T(8,128)S(1)} %broadcast_select_fusion) | data formatting | bytes 9043968 | tf_op jit(solution)/shard_map/conv_general_dilated | solution.py:33
  333.3 116.8 %all-reduce.9.cloned.1.call-done = (f32[3,3,192,192]{2,1,0,3:T(4,128)}, f32[3,3,192,192]{2,1,0,3:T(4,128)}) async-done(((f32[3,3,192,192]{2,1,0,3:T(4,128)}, f32[3,3,192,192]{2,1,0,3:T(4,128)}), (f32[3,3,192,192]{2,1,0,3:T(4,128)}, f32[3,3,192,192]{2,1,0,3:T(4,128)})) %all-reduce.9.cloned.1.call-update) | async-done | bytes 2654224
  454.2 5.3 %fusion.11 = bf16[1,16,360,192]{3,1,2,0:T(8,128)(2,1)} fusion(f32[16,1,368,192]{3,0,2,1:T(8,128)} %bitcast.330, bf16[1,16,360,192]{3,1,2,0:T(8,128)(2,1)S(1)} %copy-done.8), kind=kLoop, calls=%fused_computation.16 | loop fusion | flops 3317760 | bytes 8847360 | tf_op jit(solution)/shard_map/convert_element_type | solution.py:92
  459.5 4.7 copy.76
  464.2 46.3 %all-reduce.7.cloned.1.call-done = (f32[3,3,192,48]{2,1,0,3:T(4,128)}, f32[3,3,192,48]{2,1,0,3:T(4,128)}) async-done(((f32[3,3,192,48]{2,1,0,3:T(4,128)}, f32[3,3,192,48]{2,1,0,3:T(4,128)}), (f32[3,3,192,48]{2,1,0,3:T(4,128)}, f32[3,3,192,48]{2,1,0,3:T(4,128)})) %all-reduce.7.cloned.1.call-update) | async-done | bytes 663568 | tf_op jit(solution)/shard_map/psum | solution.py:99
  (167 shorter events, 134.1 us)
Async XLA Ops:
  7.2 443.0 %all-reduce.9.cloned.1.call-start = ((), (), s32[]{:S(2)}) async-start(), calls=%async_computation.1 | async-start | bytes 9437184
  9.1 66.7 %collective-permute-start.1 = (bf16[1,2,360,192]{2,3,1,0:T(8,128)(2,1)}, bf16[1,2,360,192]{2,3,1,0:T(8,128)(2,1)S(1)}, u32[]{:S(2)}, u32[]{:S(2)}) collective-permute-start(bf16[1,2,360,192]{2,3,1,0:T(8,128)(2,1)} %get-tuple-element.34), channel_id=1, source_target_pairs={{1,0},{2,1},{3,2},{4,3},{5,4},{6,5},{7,6},{9,8},{10,9},{11,10},{12... | collective-permute-start | bytes 829448 | tf_op jit(solution)/shard_map/ppermute | solution.py:17
  10.4 63.1 %collective-permute-start = (bf16[1,2,360,192]{2,3,1,0:T(8,128)(2,1)}, bf16[1,2,360,192]{2,3,1,0:T(8,128)(2,1)S(1)}, u32[]{:S(2)}, u32[]{:S(2)}) collective-permute-start(bf16[1,2,360,192]{2,3,1,0:T(8,128)(2,1)} %get-tuple-element.35), channel_id=1, source_target_pairs={{0,1},{1,2},{2,3},{3,4},{4,5},{5,6},{6,7},{8,9},{9,10},{10,11},{11... | collective-permute-start | bytes 829448 | tf_op jit(solution)/shard_map/ppermute | solution.py:15
  15.4 59.8 %collective-permute-start.5 = (bf16[1,2,360,192]{2,3,1,0:T(8,128)(2,1)}, bf16[1,2,360,192]{2,3,1,0:T(8,128)(2,1)S(1)}, u32[]{:S(2)}, u32[]{:S(2)}) collective-permute-start(bf16[1,2,360,192]{2,3,1,0:T(8,128)(2,1)} %get-tuple-element.32), channel_id=1, source_target_pairs={{1,0},{2,1},{3,2},{4,3},{5,4},{6,5},{7,6},{9,8},{10,9},{11,10},{12... | collective-permute-start | bytes 829448 | tf_op jit(solution)/shard_map/ppermute | solution.py:17
  16.7 31.3 %copy-start.2 = (bf16[1,16,360,192]{2,3,1,0:T(8,128)(2,1)S(1)}, bf16[1,16,360,192]{2,3,1,0:T(8,128)(2,1)}, u32[]{:S(2)}) copy-start(bf16[1,16,360,192]{2,3,1,0:T(8,128)(2,1)} %param.5) | copy-start | bytes 6635524
  16.7 56.3 %collective-permute-start.4 = (bf16[1,2,360,192]{2,3,1,0:T(8,128)(2,1)}, bf16[1,2,360,192]{2,3,1,0:T(8,128)(2,1)S(1)}, u32[]{:S(2)}, u32[]{:S(2)}) collective-permute-start(bf16[1,2,360,192]{2,3,1,0:T(8,128)(2,1)} %get-tuple-element.33), channel_id=1, source_target_pairs={{0,1},{1,2},{2,3},{3,4},{4,5},{5,6},{6,7},{8,9},{9,10},{10,11},{11... | collective-permute-start | bytes 829448 | tf_op jit(solution)/shard_map/ppermute | solution.py:15
  116.0 12.9 %copy-start.20 = (bf16[3,3,192,192]{2,3,1,0:T(8,128)(2,1)S(1)}, bf16[3,3,192,192]{2,3,1,0:T(8,128)(2,1)}, u32[]{:S(2)}) copy-start(bf16[3,3,192,192]{2,3,1,0:T(8,128)(2,1)} %all_gather.6) | copy-start | bytes 1990660
  116.0 12.9 %copy-start.35 = (pred[8,46]{0,1:T(8,128)(4,1)S(1)}, pred[8,46]{0,1:T(8,128)(4,1)}, u32[]{:S(2)}) copy-start(pred[8,46]{0,1:T(8,128)(4,1)} %constant.30) | copy-start | bytes 1108
  128.9 12.4 %copy-start.15 = (bf16[20,1,8,46,192]{4,2,3,0,1:T(8,128)(2,1)S(1)}, bf16[20,1,8,46,192]{4,2,3,0,1:T(8,128)(2,1)}, u32[]{:S(2)}) copy-start(bf16[20,1,8,46,192]{4,2,3,0,1:T(8,128)(2,1)} %copy.61) | copy-start | bytes 8478724
  128.9 12.3 %copy-start.22 = (bf16[3,3,192,192]{2,3,1,0:T(8,128)(2,1)S(1)}, bf16[3,3,192,192]{2,3,1,0:T(8,128)(2,1)}, u32[]{:S(2)}) copy-start(bf16[3,3,192,192]{2,3,1,0:T(8,128)(2,1)} %all_gather.7) | copy-start | bytes 1990660
  159.7 28.1 %copy-start = (bf16[16,1,360,192]{2,3,0,1:T(8,128)(2,1)}, bf16[16,1,360,192]{2,3,0,1:T(8,128)(2,1)S(1)}, u32[]{:S(2)}) copy-start(bf16[16,1,360,192]{2,3,0,1:T(8,128)(2,1)S(1)} %copy.98) | copy-start | bytes 6635524
  182.9 4.8 copy-start.32
  182.9 4.8 copy-start.33
  182.9 4.9 copy-start.6
  182.9 4.9 copy-start.26
  182.9 49.4 %collective-permute-start.6 = (bf16[1,2,360,192]{2,3,1,0:T(8,128)(2,1)}, bf16[1,2,360,192]{2,3,1,0:T(8,128)(2,1)}, u32[]{:S(2)}, u32[]{:S(2)}) collective-permute-start(bf16[1,2,360,192]{2,3,1,0:T(8,128)(2,1)} %slice_bitcast_fusion.27), channel_id=1, source_target_pairs={{0,1},{1,2},{2,3},{3,4},{4,5},{5,6},{6,7},{8,9},{9,10},{10,11},{11... | collective-permute-start | bytes 829448 | tf_op jit(solution)/shard_map/ppermute | solution.py:15
  202.7 17.7 %collective-permute-start.2 = (bf16[1,2,360,192]{2,3,1,0:T(8,128)(2,1)}, bf16[1,2,360,192]{2,3,1,0:T(8,128)(2,1)S(1)}, u32[]{:S(2)}, u32[]{:S(2)}) collective-permute-start(bf16[1,2,360,192]{2,3,1,0:T(8,128)(2,1)} %slice_bitcast_fusion.29), channel_id=1, source_target_pairs={{0,1},{1,2},{2,3},{3,4},{4,5},{5,6},{6,7},{8,9},{9,10},{10,11},{11... | collective-permute-start | bytes 829448 | tf_op jit(solution)/shard_map/ppermute | solution.py:15
  211.5 8.9 %collective-permute-start.3 = (bf16[1,2,360,192]{2,3,1,0:T(8,128)(2,1)}, bf16[1,2,360,192]{2,3,1,0:T(8,128)(2,1)}, u32[]{:S(2)}, u32[]{:S(2)}) collective-permute-start(bf16[1,2,360,192]{2,3,1,0:T(8,128)(2,1)} %slice_bitcast_fusion.28), channel_id=1, source_target_pairs={{1,0},{2,1},{3,2},{4,3},{5,4},{6,5},{7,6},{9,8},{10,9},{11,10},{12... | collective-permute-start | bytes 829448 | tf_op jit(solution)/shard_map/ppermute | solution.py:17
  216.7 15.7 %collective-permute-start.7 = (bf16[1,2,360,192]{2,3,1,0:T(8,128)(2,1)S(1)}, bf16[1,2,360,192]{2,3,1,0:T(8,128)(2,1)S(1)}, u32[]{:S(2)}, u32[]{:S(2)}) collective-permute-start(bf16[1,2,360,192]{2,3,1,0:T(8,128)(2,1)S(1)} %slice_bitcast_fusion.26), channel_id=1, source_target_pairs={{1,0},{2,1},{3,2},{4,3},{5,4},{6,5},{7,6},{9,8},{10,9},{11,10},{12... | collective-permute-start | bytes 829448 | tf_op jit(solution)/shard_map/ppermute | solution.py:17
  221.9 4.7 copy-start.3
  275.5 235.0 %all-reduce.7.cloned.1.call-start = ((), (), s32[]{:S(2)}) async-start(), calls=%async_computation | async-start | bytes 2359296 | tf_op jit(solution)/shard_map/psum | solution.py:99
  291.6 4.9 copy-start.10
  305.0 13.1 %copy-start.21 = (bf16[3,3,192,192]{2,3,1,0:T(8,128)(2,1)S(1)}, bf16[3,3,192,192]{2,3,1,0:T(8,128)(2,1)}, u32[]{:S(2)}) copy-start(bf16[3,3,192,192]{2,3,1,0:T(8,128)(2,1)} %all_gather.6) | copy-start | bytes 1990660
  333.3 120.8 %copy-start.8 = (bf16[1,16,360,192]{3,1,2,0:T(8,128)(2,1)S(1)}, bf16[1,16,360,192]{3,1,2,0:T(8,128)(2,1)}, u32[]{:S(2)}) copy-start(bf16[1,16,360,192]{3,1,2,0:T(8,128)(2,1)} %copy.58) | copy-start | bytes 6635524
  (22 other events, 53.6 us)
Sparse Core Ops, SparseCore 0:
  275.6 174.4 all-reduce.8
  454.3 56.1 all-reduce.6
where the time goes:
time: 531 us; the launch traced here: 521 us
  local copies, waits for them, and re-layouts  180 us (34%)
  waiting for transfers between devices  163 us (31%)
  matrix products  70.8 us (13%)
  blocking collectives  41.3 us (8%)
  other arithmetic  30 us (6%)
  starting transfers between devices  20.2 us (4%)
  between operations  15.7 us (3%)
    unnamed x3, waiting for transfers between devices  117 us
    conv_general_dilated x14, local copies, waits for them, and re-layouts, correlate(): lax.conv_general_dilated(padded, kernel, (1, 1), 'VALID', rhs_dilation=(2...  98.5 us
    psum x1, waiting for transfers between devices, per_device(): grad_one, grad_two = lax.psum((share_one, share_two), 'lat')  46.3 us
    conv_general_dilated x4, matrix products, correlate(): lax.conv_general_dilated(padded, kernel, (1, 1), 'VALID', rhs_dilation=(2...  41.6 us
    unnamed x87, local copies, waits for them, and re-layouts  37.6 us
    dot_general x18, matrix products, kernel_terms(): jnp.einsum('nhwc,nhwd->cd', padded[:, 2 * a:2 * a + height, 2 * b:2 * b +...  29.2 us
    all_gather x1, blocking collectives, per_device(): lax.all_gather(kernel_one, 'fsdp', axis=3, tiled=True)  21.1 us
    all_gather x1, blocking collectives, per_device(): lax.all_gather(kernel_two, 'fsdp', axis=3, tiled=True)  20.2 us
  transfers between devices with their start and end apart: 10, of which 2 were waited for; matrix products, arithmetic and copies ran while one was open for 23% of the time, Pallas kernels for 0%

commit v1 on v0

--- a/solution.py
+++ b/solution.py
@@ -77,7 +77,9 @@
     factor = 1.0 / jnp.sqrt(jnp.float32(cell_count))
     full_one, full_two = (
         lax.all_gather(kernel_one, "fsdp", axis=3, tiled=True),
-        lax.all_gather(kernel_two, "fsdp", axis=3, tiled=True),
+        jnp.concatenate(
+            lax.all_to_all(jnp.stack([kernel_two] * lax.axis_size("fsdp")), "fsdp", 0, 0), axis=3
+        ),
     )
     source_pad = padded_rows(fields)
     preact = correlate(source_pad, full_one)

time: 531 us -> 519 us (0.977)
  blocking collectives: 41.3 us -> 27.7 us
  starting transfers between devices: 20.2 us -> 28.4 us
    all_gather x1 -> x0, blocking collectives: 20.2 us -> none  [per_device(): lax.all_gather(kernel_two, 'fsdp', axis=3, tiled=True)]
    all_gather x1, blocking collectives: 21.1 us -> 27.7 us  [per_device(): lax.all_gather(kernel_one, 'fsdp', axis=3, tiled=True)]
    unnamed x87 -> x77, local copies, waits for them, and re-layouts: 37.6 us -> 38.9 us
  transfers between devices with their start and end apart: 10 -> 11, of which waited for: 2 -> 3; matrix products, arithmetic and copies ran while one was open for 23% -> 46% of each run, Pallas kernels for 0% -> 0%
where the time goes in v1:
time: 519 us; the launch traced here: 512 us
  local copies, waits for them, and re-layouts  183 us (35%)
  waiting for transfers between devices  159 us (31%)
  matrix products  71.1 us (14%)
  starting transfers between devices  28.4 us (5%)
  blocking collectives  27.7 us (5%)
  other arithmetic  27.1 us (5%)
  between operations  15.6 us (3%)
    unnamed x3, waiting for transfers between devices  112 us
    conv_general_dilated x14, local copies, waits for them, and re-layouts, correlate(): lax.conv_general_dilated(padded, kernel, (1, 1), 'VALID', rhs_dilation=(2...  103 us
    psum x1, waiting for transfers between devices, per_device(): grad_one, grad_two = lax.psum((share_one, share_two), 'lat')  46.3 us
    conv_general_dilated x4, matrix products, correlate(): lax.conv_general_dilated(padded, kernel, (1, 1), 'VALID', rhs_dilation=(2...  43.7 us
    unnamed x77, local copies, waits for them, and re-layouts  38.9 us
    all_gather x1, blocking collectives, per_device(): lax.all_gather(kernel_one, 'fsdp', axis=3, tiled=True)  27.7 us
    dot_general x18, matrix products, kernel_terms(): jnp.einsum('nhwc,nhwd->cd', padded[:, 2 * a:2 * a + height, 2 * b:2 * b +...  27.5 us
    ppermute x4, starting transfers between devices, extended(): lax.ppermute(tail, axis, [(i, (i + 1) % count) for i in range(ends)])  18.1 us
  transfers between devices with their start and end apart: 11, of which 3 were waited for; matrix products, arithmetic and copies ran while one was open for 46% of the time, Pallas kernels for 0%

profile of v1, /device:TPU:0, one launch (start us, length us, event | category | flops | bytes accessed | tf_op | source)
XLA Modules:
  0.0 512.0 jit_solution(16531133403128375211)
XLA Ops:
  16.7 5.8 %collective-permute-start.4 = (bf16[1,2,360,192]{2,3,1,0:T(8,128)(2,1)}, bf16[1,2,360,192]{2,3,1,0:T(8,128)(2,1)}, u32[]{:S(2)}, u32[]{:S(2)}) collective-permute-start(bf16[1,2,360,192]{2,3,1,0:T(8,128)(2,1)} %get-tuple-element.33), channel_id=1, source_target_pairs={{0,1},{1,2},{2,3},{3,4},{4,5},{5,6},{6,7},{8,9},{9,10},{10,11},{11... | collective-permute-start | bytes 829448 | tf_op jit(solution)/shard_map/ppermute | solution.py:15
  24.4 4.9 all-to-all-start
  29.3 5.0 copy.45
  39.1 27.7 %all_gather.3 = bf16[3,3,192,192]{2,3,1,0:T(8,128)(2,1)S(1)} all-gather(bf16[3,3,192,48]{2,3,1,0:T(8,128)(2,1)} %param.6), channel_id=1, replica_groups=mesh['fsdp'=4,'lat'=8] {'fsdp'}, dimensions={3}, use_global_device_ids=true | all-gather | bytes 829440 | tf_op jit(solution)/shard_map/all_gather | solution.py:79
  75.1 11.7 %reshape.204 = bf16[20,1,8,46,192]{3,2,4,0,1:T(8,128)(2,1)} reshape(bf16[20,1,368,192]{2,3,0,1:T(8,128)(2,1)} %pad) | data formatting | bytes 5652480 | tf_op jit(solution)/shard_map/conv_general_dilated | solution.py:33
  86.8 11.8 %copy.48 = bf16[20,1,8,46,192]{4,2,3,0,1:T(8,128)(2,1)} copy(bf16[20,1,8,46,192]{3,2,4,0,1:T(8,128)(2,1)} %reshape.204) | data formatting | bytes 5652480 | tf_op jit(solution)/shard_map/conv_general_dilated | solution.py:33
  99.7 12.0 %multiply_convert_fusion = (bf16[16,8,46,192]{3,1,2,0:T(8,128)(2,1)S(1)}, f32[16,8,46,192]{3,1,2,0:T(8,128)}) fusion(pred[8,46]{0,1:T(8,128)(4,1)S(1)} %copy-done.30, bf16[3,3,192,192]{2,3,1,0:T(8,128)(2,1)S(1)} %all_gather.3, bf16[20,1,7,4,192]{4,2,3,0,1:T(8,128)(2,1)S(1)} %slice.162, bf16[20,1,8,46,192]{4,2,3,0,1:T(8,128)(2,1)} %copy.48), kind=kOutput, calls=%fused_computation.12 | convolution fusion | flops 3922993152 | bytes 10488176 | tf_op jit(solution)/shard_map/conv_general_dilated | solution.py:33
  120.4 11.3 %reshape.206 = bf16[20,1,8,46,192]{3,2,4,0,1:T(8,128)(2,1)} reshape(bf16[20,1,368,192]{2,3,0,1:T(8,128)(2,1)} %pad.4) | data formatting | bytes 5652480 | tf_op jit(solution)/shard_map/conv_general_dilated | solution.py:33
  131.7 11.9 %copy.63 = bf16[20,1,8,46,192]{4,2,3,0,1:T(8,128)(2,1)} copy(bf16[20,1,8,46,192]{3,2,4,0,1:T(8,128)(2,1)} %reshape.206) | data formatting | bytes 5652480 | tf_op jit(solution)/shard_map/conv_general_dilated | solution.py:33
  184.6 8.5 %reshape.205 = bf16[20,1,8,46,192]{3,2,4,0,1:T(8,128)(2,1)} reshape(bf16[20,1,368,192]{2,3,0,1:T(8,128)(2,1)S(1)} %copy-done.6) | data formatting | bytes 5652480 | tf_op jit(solution)/shard_map/conv_general_dilated | solution.py:33
  193.1 11.8 %copy.57 = bf16[20,1,8,46,192]{4,2,3,0,1:T(8,128)(2,1)} copy(bf16[20,1,8,46,192]{3,2,4,0,1:T(8,128)(2,1)} %reshape.205) | data formatting | bytes 5652480 | tf_op jit(solution)/shard_map/conv_general_dilated | solution.py:33
  208.0 12.5 %fusion.9 = bf16[16,8,46,192]{3,1,2,0:T(8,128)(2,1)S(1)} fusion(f32[16,8,46,192]{3,1,2,0:T(8,128)} %get-tuple-element.37, pred[8,46]{0,1:T(8,128)(4,1)S(1)} %copy-done.30, bf16[3,3,192,192]{2,3,1,0:T(8,128)(2,1)S(1)} %bitcast.337, bf16[20,1,7,4,192]{4,2,3,0,1:T(8,128)(2,1)S(1)} %copy-done.20, bf16[20,1,8,46,192]{4,2,3,0,1:T(8,128)(2,1)} %copy.63), kind=kOutput, calls=%fused_computation.11 | convolution fusion | flops 3929776128 | bytes 10488176 | tf_op jit(solution)/shard_map/conv_general_dilated | solution.py:33
  245.0 7.9 %collective-permute-start.6 = (bf16[1,2,360,192]{2,3,1,0:T(8,128)(2,1)}, bf16[1,2,360,192]{2,3,1,0:T(8,128)(2,1)}, u32[]{:S(2)}, u32[]{:S(2)}) collective-permute-start(bf16[1,2,360,192]{2,3,1,0:T(8,128)(2,1)} %slice_bitcast_fusion.27), channel_id=1, source_target_pairs={{0,1},{1,2},{2,3},{3,4},{4,5},{5,6},{6,7},{8,9},{9,10},{10,11},{11... | collective-permute-start | bytes 829448 | tf_op jit(solution)/shard_map/ppermute | solution.py:15
  266.0 10.2 %broadcast_select_fusion.1 = f32[16,8,46,192]{3,1,2,0:T(8,128)S(1)} fusion(pred[8,46]{0,1:T(8,128)(4,1)S(1)} %copy-done.30, bf16[3,3,192,192]{2,3,1,0:T(8,128)(2,1)S(1)} %bitcast.338, bf16[20,1,7,4,192]{4,2,3,0,1:T(8,128)(2,1)} %slice.168, bf16[20,1,8,46,192]{4,2,3,0,1:T(8,128)(2,1)} %copy.57), kind=kOutput, calls=%fused_computation.49 | convolution fusion | flops 3917340672 | bytes 8227184 | tf_op jit(solution)/shard_map/conv_general_dilated | solution.py:33
  282.3 4.7 copy.77
  287.0 5.0 fusion.43
  292.4 8.6 %reshape.207 = bf16[20,1,8,46,192]{3,2,4,0,1:T(8,128)(2,1)} reshape(bf16[20,1,368,192]{2,3,0,1:T(8,128)(2,1)S(1)} %pad.6) | data formatting | bytes 5652480 | tf_op jit(solution)/shard_map/conv_general_dilated | solution.py:33
  301.0 12.1 %copy.72 = bf16[20,1,8,46,192]{4,2,3,0,1:T(8,128)(2,1)} copy(bf16[20,1,8,46,192]{3,2,4,0,1:T(8,128)(2,1)} %reshape.207) | data formatting | bytes 5652480 | tf_op jit(solution)/shard_map/conv_general_dilated | solution.py:33
  314.1 9.1 %broadcast_select_fusion = f32[16,8,46,192]{3,1,2,0:T(8,128)S(1)} fusion(pred[8,46]{0,1:T(8,128)(4,1)S(1)} %copy-done.30, bf16[3,3,192,192]{2,3,1,0:T(8,128)(2,1)S(1)} %copy-done.18, bf16[20,1,7,4,192]{4,2,3,0,1:T(8,128)(2,1)S(1)} %slice.178, bf16[20,1,8,46,192]{4,2,3,0,1:T(8,128)(2,1)} %copy.72), kind=kOutput, calls=%fused_computation.48 | convolution fusion | flops 3917340672 | bytes 8227184 | tf_op jit(solution)/shard_map/conv_general_dilated | solution.py:33
  323.2 6.1 %copy.73 = f32[16,8,46,192]{3,0,2,1:T(8,128)} copy(f32[16,8,46,192]{3,1,2,0:T(8,128)S(1)} %broadcast_select_fusion) | data formatting | bytes 9043968 | tf_op jit(solution)/shard_map/conv_general_dilated | solution.py:33
  329.2 111.6 %all-reduce.9.cloned.1.call-done = (f32[3,3,192,192]{2,1,0,3:T(4,128)}, f32[3,3,192,192]{2,1,0,3:T(4,128)}) async-done(((f32[3,3,192,192]{2,1,0,3:T(4,128)}, f32[3,3,192,192]{2,1,0,3:T(4,128)}), (f32[3,3,192,192]{2,1,0,3:T(4,128)}, f32[3,3,192,192]{2,1,0,3:T(4,128)})) %all-reduce.9.cloned.1.call-update) | async-done | bytes 2654224
  444.8 5.4 %fusion.11 = bf16[1,16,360,192]{3,1,2,0:T(8,128)(2,1)} fusion(f32[16,1,368,192]{3,0,2,1:T(8,128)} %bitcast.333, bf16[1,16,360,192]{3,1,2,0:T(8,128)(2,1)S(1)} %copy-done.4), kind=kLoop, calls=%fused_computation.16 | loop fusion | flops 3317760 | bytes 8847360 | tf_op jit(solution)/shard_map/convert_element_type | solution.py:94
  450.2 4.7 copy.78
  454.9 46.3 %all-reduce.7.cloned.1.call-done = (f32[3,3,192,48]{2,1,0,3:T(4,128)}, f32[3,3,192,48]{2,1,0,3:T(4,128)}) async-done(((f32[3,3,192,48]{2,1,0,3:T(4,128)}, f32[3,3,192,48]{2,1,0,3:T(4,128)}), (f32[3,3,192,48]{2,1,0,3:T(4,128)}, f32[3,3,192,48]{2,1,0,3:T(4,128)})) %all-reduce.7.cloned.1.call-update) | async-done | bytes 663568 | tf_op jit(solution)/shard_map/psum | solution.py:101
  (160 shorter events, 130.0 us)
Async XLA Ops:
  9.1 60.3 %collective-permute-start.1 = (bf16[1,2,360,192]{2,3,1,0:T(8,128)(2,1)}, bf16[1,2,360,192]{2,3,1,0:T(8,128)(2,1)}, u32[]{:S(2)}, u32[]{:S(2)}) collective-permute-start(bf16[1,2,360,192]{2,3,1,0:T(8,128)(2,1)} %get-tuple-element.34), channel_id=1, source_target_pairs={{1,0},{2,1},{3,2},{4,3},{5,4},{6,5},{7,6},{9,8},{10,9},{11,10},{12... | collective-permute-start | bytes 829448 | tf_op jit(solution)/shard_map/ppermute | solution.py:17
  10.4 56.5 %collective-permute-start = (bf16[1,2,360,192]{2,3,1,0:T(8,128)(2,1)}, bf16[1,2,360,192]{2,3,1,0:T(8,128)(2,1)S(1)}, u32[]{:S(2)}, u32[]{:S(2)}) collective-permute-start(bf16[1,2,360,192]{2,3,1,0:T(8,128)(2,1)} %get-tuple-element.35), channel_id=1, source_target_pairs={{0,1},{1,2},{2,3},{3,4},{4,5},{5,6},{6,7},{8,9},{9,10},{10,11},{11... | collective-permute-start | bytes 829448 | tf_op jit(solution)/shard_map/ppermute | solution.py:15
  15.4 99.6 %collective-permute-start.5 = (bf16[1,2,360,192]{2,3,1,0:T(8,128)(2,1)}, bf16[1,2,360,192]{2,3,1,0:T(8,128)(2,1)}, u32[]{:S(2)}, u32[]{:S(2)}) collective-permute-start(bf16[1,2,360,192]{2,3,1,0:T(8,128)(2,1)} %get-tuple-element.32), channel_id=1, source_target_pairs={{1,0},{2,1},{3,2},{4,3},{5,4},{6,5},{7,6},{9,8},{10,9},{11,10},{12... | collective-permute-start | bytes 829448 | tf_op jit(solution)/shard_map/ppermute | solution.py:17
  16.7 95.0 %collective-permute-start.4 = (bf16[1,2,360,192]{2,3,1,0:T(8,128)(2,1)}, bf16[1,2,360,192]{2,3,1,0:T(8,128)(2,1)}, u32[]{:S(2)}, u32[]{:S(2)}) collective-permute-start(bf16[1,2,360,192]{2,3,1,0:T(8,128)(2,1)} %get-tuple-element.33), channel_id=1, source_target_pairs={{0,1},{1,2},{2,3},{3,4},{4,5},{5,6},{6,7},{8,9},{9,10},{10,11},{11... | collective-permute-start | bytes 829448 | tf_op jit(solution)/shard_map/ppermute | solution.py:15
  24.4 182.4 %all-to-all-start = ((bf16[4,3,3,192,48]{3,4,2,1,0:T(8,128)(2,1)}), bf16[4,3,3,192,48]{3,4,2,1,0:T(8,128)(2,1)}, u32[]{:S(2)}, u32[]{:S(2)}) async-start(bf16[4,3,3,192,48]{3,4,2,1,0:T(8,128)(2,1)} %stack.103), calls=%async_computation | async-start | bytes 1769472 | tf_op jit(solution)/shard_map/all_to_all | solution.py:81
  29.3 5.1 copy-start
  29.3 411.5 %all-reduce.9.cloned.1.call-start = ((), (), s32[]{:S(2)}) async-start(), calls=%async_computation.2 | async-start | bytes 9437184
  66.8 32.8 %copy-start.17 = (bf16[3,3,192,192]{2,3,1,0:T(8,128)(2,1)}, bf16[3,3,192,192]{2,3,1,0:T(8,128)(2,1)S(1)}, u32[]{:S(2)}) copy-start(bf16[3,3,192,192]{2,3,1,0:T(8,128)(2,1)S(1)} %all_gather.3) | copy-start | bytes 1990660
  86.8 12.9 %copy-start.30 = (pred[8,46]{0,1:T(8,128)(4,1)S(1)}, pred[8,46]{0,1:T(8,128)(4,1)}, u32[]{:S(2)}) copy-start(pred[8,46]{0,1:T(8,128)(4,1)} %constant.30) | copy-start | bytes 1108
  152.8 8.9 %collective-permute-start.2 = (bf16[1,2,360,192]{2,3,1,0:T(8,128)(2,1)}, bf16[1,2,360,192]{2,3,1,0:T(8,128)(2,1)S(1)}, u32[]{:S(2)}, u32[]{:S(2)}) collective-permute-start(bf16[1,2,360,192]{2,3,1,0:T(8,128)(2,1)} %slice_bitcast_fusion.29), channel_id=1, source_target_pairs={{0,1},{1,2},{2,3},{3,4},{4,5},{5,6},{6,7},{8,9},{9,10},{10,11},{11... | collective-permute-start | bytes 829448 | tf_op jit(solution)/shard_map/ppermute | solution.py:15
  157.9 4.5 collective-permute-start.3
  179.0 5.6 %copy-start.6 = (bf16[20,1,368,192]{2,3,0,1:T(8,128)(2,1)S(1)}, bf16[20,1,368,192]{2,3,0,1:T(8,128)(2,1)}, u32[]{:S(2)}) copy-start(bf16[20,1,368,192]{2,3,0,1:T(8,128)(2,1)} %pad.2) | copy-start | bytes 8478724
  193.1 14.9 %copy-start.20 = (bf16[20,1,7,4,192]{4,2,3,0,1:T(8,128)(2,1)S(1)}, bf16[20,1,7,4,192]{4,2,3,0,1:T(8,128)(2,1)}, u32[]{:S(2)}) copy-start(bf16[20,1,7,4,192]{4,2,3,0,1:T(8,128)(2,1)} %slice.172) | copy-start | bytes 645124
  208.0 12.5 %copy-start.15 = (bf16[4,3,3,192,48]{3,4,0,2,1:T(8,128)(2,1)}, bf16[4,3,3,192,48]{3,4,0,2,1:T(8,128)(2,1)S(1)}, u32[]{:S(2)}) copy-start(bf16[4,3,3,192,48]{3,4,0,2,1:T(8,128)(2,1)S(1)} %copy.58) | copy-start | bytes 1990660
  224.3 4.2 copy-start.12
  244.9 10.5 %copy-start.27 = (f32[1,192,192]{2,1,0:T(8,128)S(1)}, f32[1,192,192]{2,1,0:T(8,128)}, u32[]{:S(2)}) copy-start(f32[1,192,192]{2,1,0:T(8,128)} %fusion.166) | copy-start | bytes 442372
  244.9 10.5 %copy-start.28 = (f32[1,192,192]{2,1,0:T(8,128)S(1)}, f32[1,192,192]{2,1,0:T(8,128)}, u32[]{:S(2)}) copy-start(f32[1,192,192]{2,1,0:T(8,128)} %fusion.156) | copy-start | bytes 442372
  244.9 10.5 %copy-start.3 = (bf16[1,16,360,192]{2,3,1,0:T(8,128)(2,1)S(1)}, bf16[1,16,360,192]{2,3,1,0:T(8,128)(2,1)}, u32[]{:S(2)}) copy-start(bf16[1,16,360,192]{2,3,1,0:T(8,128)(2,1)} %param.4) | copy-start | bytes 6635524
  244.9 10.5 %copy-start.22 = (bf16[1,2,360,192]{2,3,1,0:T(8,128)(2,1)S(1)}, bf16[1,2,360,192]{2,3,1,0:T(8,128)(2,1)}, u32[]{:S(2)}) copy-start(bf16[1,2,360,192]{2,3,1,0:T(8,128)(2,1)} %copy-done.21) | copy-start | bytes 829444
  245.0 42.1 %collective-permute-start.6 = (bf16[1,2,360,192]{2,3,1,0:T(8,128)(2,1)}, bf16[1,2,360,192]{2,3,1,0:T(8,128)(2,1)}, u32[]{:S(2)}, u32[]{:S(2)}) collective-permute-start(bf16[1,2,360,192]{2,3,1,0:T(8,128)(2,1)} %slice_bitcast_fusion.27), channel_id=1, source_target_pairs={{0,1},{1,2},{2,3},{3,4},{4,5},{5,6},{6,7},{8,9},{9,10},{10,11},{11... | collective-permute-start | bytes 829448 | tf_op jit(solution)/shard_map/ppermute | solution.py:15
  264.3 22.7 %collective-permute-start.7 = (bf16[1,2,360,192]{2,3,1,0:T(8,128)(2,1)}, bf16[1,2,360,192]{2,3,1,0:T(8,128)(2,1)S(1)}, u32[]{:S(2)}, u32[]{:S(2)}) collective-permute-start(bf16[1,2,360,192]{2,3,1,0:T(8,128)(2,1)} %slice_bitcast_fusion.26), channel_id=1, source_target_pairs={{1,0},{2,1},{3,2},{4,3},{5,4},{6,5},{7,6},{9,8},{10,9},{11,10},{12... | collective-permute-start | bytes 829448 | tf_op jit(solution)/shard_map/ppermute | solution.py:17
  265.8 235.3 %all-reduce.7.cloned.1.call-start = ((), (), s32[]{:S(2)}) async-start(), calls=%async_computation.1 | async-start | bytes 2359296 | tf_op jit(solution)/shard_map/psum | solution.py:101
  301.0 13.1 %copy-start.18 = (bf16[3,3,192,192]{2,3,1,0:T(8,128)(2,1)S(1)}, bf16[3,3,192,192]{2,3,1,0:T(8,128)(2,1)}, u32[]{:S(2)}) copy-start(bf16[3,3,192,192]{2,3,1,0:T(8,128)(2,1)} %copy-done.17) | copy-start | bytes 1990660
  329.2 115.6 %copy-start.4 = (bf16[1,16,360,192]{3,1,2,0:T(8,128)(2,1)S(1)}, bf16[1,16,360,192]{3,1,2,0:T(8,128)(2,1)}, u32[]{:S(2)}) copy-start(bf16[1,16,360,192]{3,1,2,0:T(8,128)(2,1)} %copy.60) | copy-start | bytes 6635524
  (18 other events, 43.3 us)
Sparse Core Ops, SparseCore 0:
  265.9 174.8 all-reduce.8
  444.9 56.1 all-reduce.6
